TPU v7x, 32 devices: a whole 2x2x4 slice. The times are simulated.
32 devices in a mesh: tok: 8 (over y, x, core), feat: 4 (over z).
Axes of the slice: x: 2, y: 2, z: 4, core: 2. Of those that a mesh axis runs over, the one named last changes fastest.
Arguments:
- entering: bfloat16 [2560, 8192], P('feat', 'tok'), may hold values from -210 to 210
- leaving: bfloat16 [2560, 8192], P('feat', 'tok'), may hold values from -280 to 280
Outputs:
- transform: float32 [2560, 2560], P('feat', 'tok')
All inputs are finite; a program needn't handle non-finite values.
Results may differ from a plain program's by a relative error of at most 0.00052.
Values may be sent and summed in bfloat16 or wider, within the bound.
A program may use at most 64 MiB of HBM per device.

v0:
```python
import jax
import jax.numpy as jnp
from jax import lax
from jax.sharding import PartitionSpec as P

ITERS = 2


ridge_share = 0.2


def token_product(left, right):
    return lax.dot_general(
        left, right, (((1,), (1,)), ((), ())), preferred_element_type=jnp.float32
    )


def body(entering, leaving):
    row_count = entering.shape[0]
    order_all = row_count * lax.axis_size("feat")
    token_total = entering.shape[1] * lax.axis_size("tok")
    gram_piece = token_product(entering, lax.all_gather(entering, "feat", axis=0, tiled=True))
    cross_piece = token_product(entering, lax.all_gather(leaving, "feat", axis=0, tiled=True))
    gram_rows = lax.psum(gram_piece, "tok")
    cross_tile = lax.psum_scatter(cross_piece, "tok", scatter_dimension=1, tiled=True)
    row_peak = jnp.max(jnp.sum(jnp.abs(gram_rows), axis=1))
    own_squares = jnp.sum(jnp.square(entering.astype(jnp.float32)))
    energy = lax.psum(own_squares, ("tok", "feat"))
    peak_all = lax.pmax(row_peak, "feat")
    ridge_term = ridge_share * energy / (token_total * order_all)
    upper_bound = peak_all / token_total + ridge_term
    center = (upper_bound + ridge_term) / 2.0
    half_span = (upper_bound - ridge_term) / 2.0
    target = cross_tile / token_total
    transform = target / center
    update = transform
    ratio_now = half_span / center
    for sweep in range(ITERS):
        iterate_half = transform.astype(jnp.bfloat16)
        applied = jnp.dot(
            gram_rows,
            lax.all_gather(iterate_half, "feat", axis=0, tiled=True).astype(jnp.float32),
            precision=lax.Precision.HIGHEST,
        )
        residual_now = target - (
            applied / token_total + ridge_term * iterate_half.astype(jnp.float32)
        )
        ratio_next = 1.0 / (2.0 * center / half_span - ratio_now)
        update = ratio_next * ratio_now * update + 2.0 * ratio_next / half_span * residual_now
        transform = transform + update
        ratio_now = ratio_next
    return transform


def solution(mesh):
    in_specs = (P("feat", "tok"), P("feat", "tok"))
    out_specs = P("feat", "tok")
    return jax.shard_map(body, mesh=mesh, in_specs=in_specs, out_specs=out_specs, check_vma=False)
```

profile of v0, /device:TPU:9, one launch (start us, length us, event | category | flops | bytes accessed | tf_op | source)
XLA Modules:
  0.0 482.4 jit_solution(17026023610516626987)
XLA Ops:
  6.5 0.0 all-gather.7.cloned.1.call-start
  6.5 0.7 all-gather.7.cloned.1.call-update
  7.3 0.0 all-gather.5.cloned.1.call-start
  7.3 0.7 all-gather.5.cloned.1.call-update
  8.0 0.0 all-reduce.2.cloned.1.call-start
  8.1 97.3 %all-gather.7.cloned.1.call-done = bf16[2560,1024]{1,0:T(8,128)(2,1)} async-done(((bf16[640,1024]{1,0:T(8,128)(2,1)}), bf16[2560,1024]{1,0:T(8,128)(2,1)}) %all-gather.7.cloned.1.call-update) | async-done | bytes 5242896 | tf_op jit(solution)/shard_map/all_gather | solution.py:22
  105.3 9.2 %fusion.13 = f32[640,2560]{1,0:T(8,128)} fusion(bf16[640,1024]{1,0:T(8,128)(2,1)} %param.2, bf16[2560,1024]{1,0:T(8,128)(2,1)} %all-gather.7.cloned.1.call-done), kind=kOutput, calls=%fused_computation.18 | convolution fusion | flops 3355443200 | bytes 13107200 | tf_op jit(solution)/shard_map/dot_general | solution.py:13
  114.5 0.0 copy-start
  114.5 0.0 all-reduce.2.cloned.1.call-update
  114.6 0.0 reduce-scatter.2.cloned.1.call-start
  114.6 88.7 %all-gather.5.cloned.1.call-done = bf16[2560,1024]{1,0:T(8,128)(2,1)} async-done(((bf16[640,1024]{1,0:T(8,128)(2,1)}), bf16[2560,1024]{1,0:T(8,128)(2,1)}) %all-gather.5.cloned.1.call-update) | async-done | bytes 5242896 | tf_op jit(solution)/shard_map/all_gather | solution.py:23
  203.3 0.0 copy-done
  203.3 9.4 %fusion.12 = f32[640,2560]{0,1:T(8,128)} fusion(bf16[640,1024]{1,0:T(8,128)(2,1)S(1)} %copy-done, bf16[2560,1024]{1,0:T(8,128)(2,1)} %all-gather.5.cloned.1.call-done), kind=kOutput, calls=%fused_computation.17 | convolution fusion | flops 3355443200 | bytes 13107200 | tf_op jit(solution)/shard_map/dot_general | solution.py:13
  212.8 0.0 reduce-scatter.2.cloned.1.call-update
  212.8 0.0 all-gather.9.cloned.1.call-start
  212.8 1.3 multiply_reduce_fusion
  214.1 43.9 %psum.15 = f32[]{:T(128)} all-reduce(f32[]{:T(128)} %multiply_reduce_fusion), channel_id=1, replica_groups=mesh['tok'=8,'feat'=4] {'tok','feat'}, use_global_device_ids=true, to_apply=%region_6.0 | all-reduce | flops 1 | bytes 8 | tf_op jit(solution)/shard_map/psum | solution.py:28
  258.0 57.5 %all-reduce.2.cloned.1.call-done = f32[640,2560]{1,0:T(8,128)} async-done(((f32[640,2560]{1,0:T(8,128)}), f32[640,2560]{1,0:T(8,128)}) %all-reduce.2.cloned.1.call-update) | async-done | bytes 6553616 | tf_op jit(solution)/shard_map/psum | solution.py:24
  315.5 3.4 abs_reduce_fusion
  318.9 0.6 reduce_max.9
  320.2 7.5 %pmax.7 = f32[]{:T(128)} all-reduce(f32[]{:T(128)} %reduce_max.9), channel_id=1, replica_groups=mesh['tok'=8,'feat'=4] {'feat'}, use_global_device_ids=true, to_apply=%region_4.0 | all-reduce | flops 1 | bytes 8 | tf_op jit(solution)/shard_map/pmax | solution.py:29
  328.4 53.7 %reduce-scatter.2.cloned.1.call-done = f32[640,320]{0,1:T(8,128)} async-done(((f32[640,2560]{0,1:T(8,128)}), f32[640,320]{0,1:T(8,128)}) %reduce-scatter.2.cloned.1.call-update) | async-done | bytes 819216 | tf_op jit(solution)/shard_map/reduce_scatter | solution.py:25
  382.1 2.0 fusion.10
  384.1 0.0 all-gather.9.cloned.1.call-update
  384.1 0.2 all-gather.11.cloned.1.call-start
  384.5 0.0 copy-start.1
  384.5 36.8 %all-gather.9.cloned.1.call-done = bf16[2560,320]{0,1:T(8,128)(2,1)} async-done(((bf16[640,320]{0,1:T(8,128)(2,1)}), bf16[2560,320]{0,1:T(8,128)(2,1)}) %all-gather.9.cloned.1.call-update) | async-done | bytes 1638416 | tf_op jit(solution)/shard_map/all_gather | solution.py:42
  421.3 8.5 %fusion.11 = (bf16[640,320]{0,1:T(8,128)(2,1)}, f32[640,320]{0,1:T(8,128)S(1)}) fusion(f32[]{:T(128)S(6)} %div.49, f32[640,320]{0,1:T(8,128)} %reduce-scatter.2.cloned.1.call-done, f32[]{:T(128)S(6)} %div.48, f32[640,2560]{1,0:T(8,128)} %all-reduce.2.cloned.1.call-done, bf16[2560,320]{0,1:T(8,128)(2,1)} %all-gather.9.cloned.1.call-done, f32[]{:T(128)S(6)} %div.56, ...), kind=kOutput, calls=%fused_computation.16 | convolution fusion | flops 6294118400 | bytes 10240016 | tf_op jit(solution)/shard_map/dot_general | solution.py:40
  429.9 0.0 all-gather.11.cloned.1.call-update
  430.0 37.1 %all-gather.11.cloned.1.call-done = bf16[2560,320]{0,1:T(8,128)(2,1)} async-done(((bf16[640,320]{0,1:T(8,128)(2,1)}), bf16[2560,320]{0,1:T(8,128)(2,1)}) %all-gather.11.cloned.1.call-update) | async-done | bytes 1638416 | tf_op jit(solution)/shard_map/all_gather | solution.py:42
  467.1 0.0 copy-done.1
  467.1 8.5 %fusion.7 = f32[640,320]{0,1:T(8,128)} fusion(f32[640,2560]{1,0:T(8,128)} %all-reduce.2.cloned.1.call-done, bf16[2560,320]{0,1:T(8,128)(2,1)} %all-gather.11.cloned.1.call-done, f32[640,320]{0,1:T(8,128)S(1)} %get-tuple-element.6, f32[640,320]{0,1:T(8,128)S(1)} %copy-done.1, f32[]{:T(128)S(6)} %div.59, f32[]{:T(128)S(6)} %mul.56, f32[]{:T(128)S(6)} %div.48, ...), kind=kOutput, calls=%fused_computation.11 | convolution fusion | flops 6294118400 | bytes 10649616 | tf_op jit(solution)/shard_map/dot_general | solution.py:40
Async XLA Ops:
  6.5 98.8 %all-gather.7.cloned.1.call-start = ((), (), s32[]{:S(2)}) async-start(), calls=%async_computation.3 | async-start | bytes 6553600 | tf_op jit(solution)/shard_map/all_gather | solution.py:22
  7.3 196.1 %all-gather.5.cloned.1.call-start = ((), (), s32[]{:S(2)}) async-start(), calls=%async_computation.1 | async-start | bytes 6553600 | tf_op jit(solution)/shard_map/all_gather | solution.py:23
  8.0 307.5 %all-reduce.2.cloned.1.call-start = ((), (), s32[]{:S(2)}) async-start(), calls=%async_computation.4 | async-start | bytes 13107200 | tf_op jit(solution)/shard_map/psum | solution.py:24
  114.5 88.8 %copy-start = (bf16[640,1024]{1,0:T(8,128)(2,1)S(1)}, bf16[640,1024]{1,0:T(8,128)(2,1)}, u32[]{:S(2)}) copy-start(bf16[640,1024]{1,0:T(8,128)(2,1)} %param.2) | copy-start | bytes 3932164
  114.6 267.6 %reduce-scatter.2.cloned.1.call-start = ((), (), s32[]{:S(2)}) async-start(), calls=%async_computation.2 | async-start | bytes 7372800 | tf_op jit(solution)/shard_map/reduce_scatter | solution.py:25
  212.8 208.6 %all-gather.9.cloned.1.call-start = ((), (), s32[]{:S(2)}) async-start(), calls=%async_computation.5 | async-start | bytes 2048000 | tf_op jit(solution)/shard_map/all_gather | solution.py:42
  384.1 83.0 %all-gather.11.cloned.1.call-start = ((), (), s32[]{:S(2)}) async-start(), calls=%async_computation.6 | async-start | bytes 2048000 | tf_op jit(solution)/shard_map/all_gather | solution.py:42
  384.5 82.6 %copy-start.1 = (f32[640,320]{0,1:T(8,128)S(1)}, f32[640,320]{0,1:T(8,128)}, u32[]{:S(2)}) copy-start(f32[640,320]{0,1:T(8,128)} %reduce-scatter.2.cloned.1.call-done) | copy-start | bytes 2457604
Sparse Core Ops, SparseCore 0:
  8.9 96.4 all-gather.6
  106.9 96.3 all-gather.4
  206.6 108.8 all-reduce.1
  318.8 63.2 reduce-scatter.1
  384.2 37.0 all-gather.8
  430.0 36.9 all-gather.10
where the time goes:
time: 485 us; the launch traced here: 482 us
  waiting for transfers between devices  373 us (77%)
  blocking collectives  51.4 us (11%)
  matrix products  35.6 us (7%)
  between operations  15 us (3%)
  other arithmetic  7.24 us (1%)
    all_gather x1, waiting for transfers between devices, body(): lax.all_gather(entering, 'feat', axis=0, tiled=True)  97.3 us
    all_gather x1, waiting for transfers between devices, body(): lax.all_gather(leaving, 'feat', axis=0, tiled=True)  88.7 us
    all_gather x2, waiting for transfers between devices, body(): lax.all_gather(iterate_half, 'feat', axis=0, tiled=True).astype(jnp.float32)  73.9 us
    psum x1, waiting for transfers between devices, body(): gram_rows = lax.psum(gram_piece, 'tok')  57.5 us
    reduce_scatter x1, waiting for transfers between devices, body(): lax.psum_scatter(cross_piece, 'tok', scatter_dimension=1, tiled=True)  53.7 us
    psum x1, blocking collectives, body(): energy = lax.psum(own_squares, ('tok', 'feat'))  43.9 us
    dot_general x2, matrix products, token_product(): lax.dot_general(left, right, (((1,), (1,)), ((), ())), preferred_element_...  18.6 us
    dot_general x2, matrix products, body(): jnp.dot(gram_rows, lax.all_gather(iterate_half, 'feat', axis=0, tiled=Tru...  17 us
  transfers between devices with their start and end apart: 6, of which 6 were waited for; matrix products, arithmetic and copies ran while one was open for 5% of the time, Pallas kernels for 0%

commit v1 on v0

--- a/solution.py
+++ b/solution.py
@@ -1,12 +1,18 @@
+import functools
+
 import jax
 import jax.numpy as jnp
 from jax import lax
+from jax.experimental import pallas as pl
+from jax.experimental.pallas import tpu as pltpu
 from jax.sharding import PartitionSpec as P
 
 ITERS = 2
 
-
 ridge_share = 0.2
+
+MESH = pl.DeviceIdType.MESH
+VMEM_BYTES = 64000 * 1024
 
 
 def token_product(left, right):
@@ -15,7 +21,7 @@
     )
 
 
-def body(entering, leaving):
+def plain_body(entering, leaving):
     row_count = entering.shape[0]
     order_all = row_count * lax.axis_size("feat")
     token_total = entering.shape[1] * lax.axis_size("tok")
@@ -52,7 +58,401 @@
     return transform
 
 
+def kernel(
+    n_tok, n_feat,
+    e_ref, l_ref, out_ref,
+    eall, part, sib, recv, gall, glow, cbuf, ubuf, tbuf, tfull, stat, zstat, fin, halves, outs,
+    load_sem, up_sem, down_sem, ag_sem, sib_ssem, sib_rsem, rs_ssem, rs_rsem,
+    g_ssem, g_rsem, gl_ssem, gl_rsem, st_ssem, st_rsem, zs_ssem, zs_rsem,
+    tg_ssem, tg_rsem, tf_ssem, tf_rsem, fa_ssem, fa_rsem, fb_ssem, fb_rsem,
+):
+    f32, bf16 = jnp.float32, jnp.bfloat16
+    t = lax.axis_index("tok")
+    z = lax.axis_index("feat")
+    chips = n_tok // 2
+    p, c = t // 2, t % 2
+    mate = 2 * p + 1 - c
+    rows, tokens = e_ref.shape
+    sub = rows // n_tok
+    token_total = tokens * n_tok
+    order_all = rows * n_feat
+    width = rows // 2
+
+    load = pltpu.make_async_copy(e_ref, eall.at[z], load_sem)
+    load.start()
+
+    barrier = pltpu.get_barrier_semaphore()
+    for d in range(1, n_tok):
+        pl.semaphore_signal(
+            barrier, inc=1, device_id=(lax.rem(t + d, n_tok), z), device_id_type=MESH
+        )
+    for d in range(1, n_feat):
+        pl.semaphore_signal(
+            barrier, inc=1, device_id=(t, lax.rem(z + d, n_feat)), device_id_type=MESH
+        )
+    load.wait()
+    pl.semaphore_wait(barrier, n_tok + n_feat - 2)
+
+    def remote(src, dst, ssem, rsem, tok, feat):
+        return pltpu.make_async_remote_copy(
+            src_ref=src, dst_ref=dst, send_sem=ssem, recv_sem=rsem,
+            device_id=(tok, feat), device_id_type=MESH,
+        )
+
+    def up_copy(r):
+        return remote(eall.at[r], eall.at[r], up_sem.at[r], ag_sem.at[r], t, z + 1)
+
+    def down_copy(r):
+        return remote(eall.at[r], eall.at[r], down_sem.at[r], ag_sem.at[r], t, z - 1)
+
+    def sib_copy(r):
+        return remote(part.at[r, 1 - c], sib.at[r], sib_ssem.at[r], sib_rsem.at[r], mate, z)
+
+    def rs_copy(r, d):
+        dest = lax.rem(p + d, chips)
+        return remote(
+            part.at[r, c, dest], recv.at[d - 1, r], rs_ssem.at[r, d - 1], rs_rsem.at[r, d - 1],
+            2 * dest + c, z,
+        )
+
+    def fetch(r, first):
+        @pl.when(jnp.logical_not(first))
+        def _():
+            down_copy(r).wait_recv()
+
+        @pl.when(jnp.logical_and(r <= z, z < n_feat - 1))
+        def _():
+            up_copy(r).start()
+
+        @pl.when(jnp.logical_and(r >= z, z > 0))
+        def _():
+            down_copy(r).start()
+
+    def process(r):
+        def chip_rows(q, carry):
+            at = pl.multiple_of(q * 2 * sub, 2 * sub)
+            block = eall[r, pl.ds(at, 2 * sub), :]
+            gram = token_product(block, e_ref[...])
+            part[r, 0, q, 0] = gram[:sub]
+            part[r, 1, q, 0] = gram[sub:]
+            cross = token_product(block, l_ref[...])
+            part[r, 0, q, 1] = cross[:sub]
+            part[r, 1, q, 1] = cross[sub:]
+            return carry
+
+        lax.fori_loop(0, chips, chip_rows, 0)
+        sib_copy(r).start()
+
+    def finish(r):
+        sib_copy(r).wait_recv()
+
+        def add(q, carry):
+            part[r, c, q] = part[r, c, q] + sib[r, q]
+            return carry
+
+        lax.fori_loop(0, chips, add, 0)
+        for d in range(1, chips):
+            rs_copy(r, d).start()
+
+    def both(s, action):
+        @pl.when(z - s >= 0)
+        def _():
+            action(z - s)
+
+        @pl.when(jnp.logical_and(s > 0, z + s < n_feat))
+        def _():
+            action(z + s)
+
+    def level(s, carry):
+        both(s, lambda r: fetch(r, s == 0))
+        both(s, process)
+
+        @pl.when(s > 0)
+        def _():
+            both(s - 1, finish)
+
+        return carry
+
+    lax.fori_loop(0, n_feat, level, 0)
+    both(n_feat - 1, finish)
+
+    col_abs = jnp.zeros((8, rows), f32)
+    diag = jnp.zeros((8, rows), f32)
+    row_id = lax.broadcasted_iota(jnp.int32, (sub, rows), 0)
+    col_id = lax.broadcasted_iota(jnp.int32, (sub, rows), 1)
+    on_diag = col_id == row_id + t * sub
+
+    def total(r, carry):
+        col_abs, diag = carry
+        for d in range(1, chips):
+            rs_copy(r, d).wait_recv()
+        both_sum = part[r, c, p]
+        for d in range(1, chips):
+            both_sum = both_sum + recv[d - 1, r]
+        gram = both_sum[0]
+        cbuf[r] = both_sum[1] / token_total
+        high = gram.astype(bf16)
+        gall[z, r] = high
+
+        @pl.when(r == z)
+        def _():
+            glow[z] = (gram - high.astype(f32)).astype(bf16)
+
+        col_abs = col_abs + jnp.sum(jnp.abs(gram).reshape(sub // 8, 8, rows), axis=0)
+        kept = jnp.where(on_diag, gram, 0.0) * jnp.where(r == z, 1.0, 0.0)
+        diag = diag + jnp.sum(kept.reshape(sub // 8, 8, rows), axis=0)
+        return col_abs, diag
+
+    col_abs, diag = lax.fori_loop(0, n_feat, total, (col_abs, diag))
+    stat[t, 0] = col_abs
+    stat[t, 1] = diag
+
+    def st_copy(d):
+        return remote(
+            stat.at[t], stat.at[t], st_ssem.at[d - 1], st_rsem.at[d - 1],
+            lax.rem(t + d, n_tok), z,
+        )
+
+    def g_copy(d):
+        return remote(
+            gall.at[z], gall.at[z], g_ssem.at[d - 1], g_rsem.at[d - 1],
+            t, lax.rem(z + d, n_feat),
+        )
+
+    def gl_copy(d):
+        return remote(
+            glow.at[z], glow.at[z], gl_ssem.at[d - 1], gl_rsem.at[d - 1],
+            t, lax.rem(z + d, n_feat),
+        )
+
+    def zs_copy(d):
+        return remote(
+            zstat.at[z], zstat.at[z], zs_ssem.at[d - 1], zs_rsem.at[d - 1],
+            t, lax.rem(z + d, n_feat),
+        )
+
+    for d in range(1, n_tok):
+        st_copy(d).start()
+    for d in range(1, n_tok):
+        st_copy(d).wait_recv()
+    tok_sum = jnp.sum(stat[...], axis=0)
+    sums = jnp.sum(tok_sum[0], axis=0, keepdims=True)
+    peak = jnp.max(sums, axis=1, keepdims=True)
+    trace = jnp.sum(jnp.sum(tok_sum[1], axis=0, keepdims=True), axis=1, keepdims=True)
+    zstat[z, 0] = jnp.broadcast_to(peak, (8, 128))
+    zstat[z, 1] = jnp.broadcast_to(trace, (8, 128))
+    for d in range(1, n_feat):
+        zs_copy(d).start()
+    for d in range(1, n_feat):
+        g_copy(d).start()
+        gl_copy(d).start()
+    for d in range(1, n_feat):
+        zs_copy(d).wait_recv()
+    seen = zstat[...]
+    peak_all = jnp.max(seen[:, 0], axis=0)[:1, :1]
+    energy = jnp.sum(seen[:, 1], axis=0)[:1, :1]
+    ridge_term = ridge_share * energy / (token_total * order_all)
+    upper_bound = peak_all / token_total + ridge_term
+    center = (upper_bound + ridge_term) / 2.0
+    half_span = (upper_bound - ridge_term) / 2.0
+    ratio_now = half_span / center
+
+    def start_iterate(r, carry):
+        first = cbuf[r] / center
+        tbuf[r] = first
+        ubuf[r] = first
+        tfull[0, r, t] = first.astype(bf16)
+        return carry
+
+    lax.fori_loop(0, n_feat, start_iterate, 0)
+
+    def tg_copy(it, d):
+        dest = lax.rem(p + d, chips)
+        return remote(
+            tfull.at[it, :, t], tfull.at[it, :, t], tg_ssem.at[it, d - 1], tg_rsem.at[it, d - 1],
+            2 * dest + c, z,
+        )
+
+    def tf_copy(it, d):
+        tile = 2 * lax.rem(p + chips - d, chips) + c
+        return remote(
+            tfull.at[it, :, tile], tfull.at[it, :, tile], tf_ssem.at[it, d], tf_rsem.at[it, d],
+            mate, z,
+        )
+
+    for it in range(ITERS):
+        for d in range(1, chips):
+            tg_copy(it, d).start()
+        tf_copy(it, 0).start()
+        for d in range(1, chips):
+            tg_copy(it, d).wait_recv()
+            tf_copy(it, d).start()
+        if it == 0:
+            for d in range(1, n_feat):
+                g_copy(d).wait_recv()
+                gl_copy(d).wait_recv()
+        for d in range(chips):
+            tf_copy(it, d).wait_recv()
+        ratio_next = 1.0 / (2.0 * center / half_span - ratio_now)
+        keep = ratio_next * ratio_now
+        gain = 2.0 * ratio_next / half_span
+
+        def multiply(k, carry):
+            weights = tfull[it, k].reshape(rows, rows)
+            left = gall[k].reshape(n_feat * sub, rows)
+            product = jnp.dot(left, weights, preferred_element_type=f32)
+            low = jnp.dot(glow[k], weights, preferred_element_type=f32)
+            product = product.reshape(n_feat, sub, rows)
+
+            @pl.when(k == 0)
+            def _():
+                fin[...] = product
+
+            @pl.when(k > 0)
+            def _():
+                fin[...] = fin[...] + product
+
+            recv[0, k, 0] = low
+            return carry
+
+        lax.fori_loop(0, n_feat, multiply, 0)
+
+        def advance(r, carry):
+            applied = fin[r] + recv[0, r, 0]
+            half = tfull[it, r, t].astype(f32)
+            residual = cbuf[r] - (applied / token_total + ridge_term * half)
+            update = keep * ubuf[r] + gain * residual
+            after = tbuf[r] + update
+            ubuf[r] = update
+            tbuf[r] = after
+            if it + 1 < ITERS:
+                tfull[it + 1, r, t] = after.astype(bf16)
+            return carry
+
+        lax.fori_loop(0, n_feat, advance, 0)
+        ratio_now = ratio_next
+
+    def fa_copy(d):
+        dest = lax.rem(z + d, n_feat)
+        return remote(
+            tbuf.at[dest], sib.at[0, z, 0], fa_ssem.at[d - 1], fa_rsem.at[d - 1], t, dest
+        )
+
+    def fb_copy(d):
+        dest = lax.rem(t + d, n_tok)
+        return remote(
+            halves.at[dest], outs.at[t], fb_ssem.at[d - 1], fb_rsem.at[d - 1], dest, z
+        )
+
+    for d in range(1, n_feat):
+        fa_copy(d).start()
+    sib[0, z, 0] = tbuf[z]
+    for d in range(1, n_feat):
+        fa_copy(d).wait_recv()
+    for k in range(n_feat):
+        tile = sib[0, k, 0]
+        halves[2 * k] = tile[:, :width]
+        halves[2 * k + 1] = tile[:, width:]
+    for d in range(1, n_tok):
+        fb_copy(d).start()
+    outs[t] = halves[t]
+    for d in range(1, n_tok):
+        fb_copy(d).wait_recv()
+    out_ref[...] = outs[...]
+
+    def drain(r, carry):
+        @pl.when(jnp.logical_and(r <= z, z < n_feat - 1))
+        def _():
+            up_copy(r).wait_send()
+
+        @pl.when(jnp.logical_and(r >= z, z > 0))
+        def _():
+            down_copy(r).wait_send()
+
+        sib_copy(r).wait_send()
+        for d in range(1, chips):
+            rs_copy(r, d).wait_send()
+        return carry
+
+    lax.fori_loop(0, n_feat, drain, 0)
+    for d in range(1, n_tok):
+        st_copy(d).wait_send()
+        fb_copy(d).wait_send()
+    for d in range(1, n_feat):
+        g_copy(d).wait_send()
+        gl_copy(d).wait_send()
+        zs_copy(d).wait_send()
+        fa_copy(d).wait_send()
+    for it in range(ITERS):
+        for d in range(1, chips):
+            tg_copy(it, d).wait_send()
+        for d in range(chips):
+            tf_copy(it, d).wait_send()
+
+
+def kernel_body(n_tok, n_feat, entering, leaving):
+    rows, tokens = entering.shape
+    chips, sub, width = n_tok // 2, rows // n_tok, rows // 2
+    f32, bf16 = jnp.float32, jnp.bfloat16
+    dma = pltpu.SemaphoreType.DMA
+    vmem = pltpu.VMEM
+    tile = (n_feat, sub, rows)
+    out = pl.pallas_call(
+        functools.partial(kernel, n_tok, n_feat),
+        out_shape=jax.ShapeDtypeStruct((n_tok, sub, width), f32),
+        in_specs=[pl.BlockSpec(memory_space=pltpu.VMEM)] * 2,
+        out_specs=pl.BlockSpec(memory_space=pltpu.VMEM),
+        scratch_shapes=[
+            vmem((n_feat, rows, tokens), bf16),
+            vmem((n_feat, 2, chips, 2, sub, rows), f32),
+            vmem((n_feat, chips, 2, sub, rows), f32),
+            vmem((chips - 1, n_feat, 2, sub, rows), f32),
+            vmem((n_feat, n_feat, sub, rows), bf16),
+            vmem((n_feat, sub, rows), bf16),
+            vmem(tile, f32),
+            vmem(tile, f32),
+            vmem(tile, f32),
+            vmem((ITERS, n_feat, n_tok, sub, rows), bf16),
+            vmem((n_tok, 2, 8, rows), f32),
+            vmem((n_feat, 2, 8, 128), f32),
+            vmem(tile, f32),
+            vmem((n_tok, sub, width), f32),
+            vmem((n_tok, sub, width), f32),
+            dma,
+            dma((n_feat,)), dma((n_feat,)), dma((n_feat,)),
+            dma((n_feat,)), dma((n_feat,)),
+            dma((n_feat, chips - 1)), dma((n_feat, chips - 1)),
+            dma((n_feat - 1,)), dma((n_feat - 1,)),
+            dma((n_feat - 1,)), dma((n_feat - 1,)),
+            dma((n_tok - 1,)), dma((n_tok - 1,)),
+            dma((n_feat - 1,)), dma((n_feat - 1,)),
+            dma((ITERS, chips - 1)), dma((ITERS, chips - 1)),
+            dma((ITERS, chips)), dma((ITERS, chips)),
+            dma((n_feat - 1,)), dma((n_feat - 1,)),
+            dma((n_tok - 1,)), dma((n_tok - 1,)),
+        ],
+        compiler_params=pltpu.CompilerParams(
+            collective_id=0, has_side_effects=True, vmem_limit_bytes=VMEM_BYTES
+        ),
+    )(entering, leaving)
+    return out.reshape(rows, width)
+
+
 def solution(mesh):
+    n_tok, n_feat = mesh.shape["tok"], mesh.shape["feat"]
+
+    def body(entering, leaving):
+        rows, tokens = entering.shape
+        fits = (
+            n_tok == 2 * n_feat
+            and rows % (16 * n_tok) == 0
+            and rows % 128 == 0
+            and tokens % 128 == 0
+        )
+        if fits:
+            return kernel_body(n_tok, n_feat, entering, leaving)
+        return plain_body(entering, leaving)
+
     in_specs = (P("feat", "tok"), P("feat", "tok"))
     out_specs = P("feat", "tok")
     return jax.shard_map(body, mesh=mesh, in_specs=in_specs, out_specs=out_specs, check_vma=False)

time: 485 us -> 237 us (0.49)
  waiting for transfers between devices: 373 us -> 0 us
  Pallas kernels: 0 us -> 234 us
  blocking collectives: 51.4 us -> 0 us
  matrix products: 35.6 us -> 0 us
  between operations: 15 us -> 0.01 us
  other arithmetic: 7.24 us -> 0 us
    all_gather x4 -> x0, waiting for transfers between devices: 260 us -> none  [the longest x1 97.3 us: body(): lax.all_gather(entering, 'feat', axis=0, tiled=True)]
    pallas_call x0 -> x1, Pallas kernels: none -> 234 us  [kernel_body(): pl.pallas_call(functools.partial(kernel, n_tok, n_feat), out_shape=jax.Sh...]
    psum x1 -> x0, waiting for transfers between devices: 57.5 us -> none  [body(): gram_rows = lax.psum(gram_piece, 'tok')]
    reduce_scatter x1 -> x0, waiting for transfers between devices: 53.7 us -> none  [body(): lax.psum_scatter(cross_piece, 'tok', scatter_dimension=1, tiled=True)]
    psum x1 -> x0, blocking collectives: 43.9 us -> none  [body(): energy = lax.psum(own_squares, ('tok', 'feat'))]
    dot_general x4 -> x0, matrix products: 35.6 us -> none  [the longest x2 18.6 us: token_product(): lax.dot_general(left, right, (((1,), (1,)), ((), ())), preferred_element_...]
    pmax x1 -> x0, blocking collectives: 7.52 us -> none  [body(): peak_all = lax.pmax(row_peak, 'feat')]
  transfers between devices with their start and end apart: 6 -> 0, of which waited for: 6 -> 0; matrix products, arithmetic and copies ran while one was open for 5% -> 0% of each run, Pallas kernels for 0% -> 0%
where the time goes in v1:
time: 237 us
  Pallas kernels  234 us (99%)
  local copies, waits for them, and re-layouts  2.41 us (1%)
    pallas_call x1, Pallas kernels, kernel_body(): pl.pallas_call(functools.partial(kernel, n_tok, n_feat), out_shape=jax.Sh...  234 us

profile of v1, /device:TPU:9, one launch (start us, length us, event | category | flops | bytes accessed | tf_op | source)
XLA Modules:
  0.0 236.8 jit_solution(10314495246156256728)
XLA Ops:
  0.0 234.3 %shard_map.28 = f32[8,80,320]{2,1,0:T(8,128)} custom-call(bf16[640,1024]{1,0:T(8,128)(2,1)} %e_ref.1, bf16[640,1024]{1,0:T(8,128)(2,1)} %l_ref.1), custom_call_target="tpu_custom_call" | custom-call | tf_op jit(solution)/shard_map/pallas_call | solution.py:400
  234.4 2.4 %copy.3 = f32[640,320]{0,1:T(8,128)} copy(f32[640,320]{1,0:T(8,128)} %bitcast.1) | data formatting | bytes 1638400 | tf_op jit(solution)/shard_map/reshape | solution.py:438

commit v2 on v1

--- a/solution.py
+++ b/solution.py
@@ -72,8 +72,11 @@
     chips = n_tok // 2
     p, c = t // 2, t % 2
     mate = 2 * p + 1 - c
-    rows, tokens = e_ref.shape
-    sub = rows // n_tok
+    sub, tokens = e_ref.shape[1:]
+    rows = sub * n_tok
+    cut = 16 * ((sub // 16 + 1) // 2)
+    pieces = [(0, cut), (cut, sub)]
+    group = 2 if chips % 2 == 0 else 1
     token_total = tokens * n_tok
     order_all = rows * n_feat
     width = rows // 2
@@ -99,60 +102,85 @@
             device_id=(tok, feat), device_id_type=MESH,
         )
 
-    def up_copy(r):
-        return remote(eall.at[r], eall.at[r], up_sem.at[r], ag_sem.at[r], t, z + 1)
-
-    def down_copy(r):
-        return remote(eall.at[r], eall.at[r], down_sem.at[r], ag_sem.at[r], t, z - 1)
-
-    def sib_copy(r):
-        return remote(part.at[r, 1 - c], sib.at[r], sib_ssem.at[r], sib_rsem.at[r], mate, z)
-
-    def rs_copy(r, d):
+    def up_copy(r, h):
+        at = eall.at[r, :, slice(*pieces[h])]
+        return remote(at, at, up_sem.at[r, h], ag_sem.at[r, h], t, z + 1)
+
+    def down_copy(r, h):
+        at = eall.at[r, :, slice(*pieces[h])]
+        return remote(at, at, down_sem.at[r, h], ag_sem.at[r, h], t, z - 1)
+
+    def sib_copy(r, h):
+        at = slice(*pieces[h])
+        return remote(
+            part.at[r, 1 - c, :, :, at], sib.at[r, :, :, at], sib_ssem.at[r, h],
+            sib_rsem.at[r, h], mate, z,
+        )
+
+    def rs_copy(r, h, d):
         dest = lax.rem(p + d, chips)
-        return remote(
-            part.at[r, c, dest], recv.at[d - 1, r], rs_ssem.at[r, d - 1], rs_rsem.at[r, d - 1],
-            2 * dest + c, z,
-        )
-
-    def fetch(r, first):
+        at = slice(*pieces[h])
+        return remote(
+            part.at[r, c, dest, :, at], recv.at[d - 1, r, :, at], rs_ssem.at[r, h, d - 1],
+            rs_rsem.at[r, h, d - 1], 2 * dest + c, z,
+        )
+
+    def g_copy(r, d):
+        return remote(
+            gall.at[z, r], gall.at[z, r], g_ssem.at[r, d - 1], g_rsem.at[r, d - 1],
+            t, lax.rem(z + d, n_feat),
+        )
+
+    def gl_copy(d):
+        return remote(
+            glow.at[z], glow.at[z], gl_ssem.at[d - 1], gl_rsem.at[d - 1],
+            t, lax.rem(z + d, n_feat),
+        )
+
+    def fetch(r, h, first):
         @pl.when(jnp.logical_not(first))
         def _():
-            down_copy(r).wait_recv()
+            down_copy(r, h).wait_recv()
 
         @pl.when(jnp.logical_and(r <= z, z < n_feat - 1))
         def _():
-            up_copy(r).start()
+            up_copy(r, h).start()
 
         @pl.when(jnp.logical_and(r >= z, z > 0))
         def _():
-            down_copy(r).start()
-
-    def process(r):
-        def chip_rows(q, carry):
-            at = pl.multiple_of(q * 2 * sub, 2 * sub)
-            block = eall[r, pl.ds(at, 2 * sub), :]
-            gram = token_product(block, e_ref[...])
-            part[r, 0, q, 0] = gram[:sub]
-            part[r, 1, q, 0] = gram[sub:]
+            down_copy(r, h).start()
+
+    def process(r, h):
+        lo, hi = pieces[h]
+        size = hi - lo
+        own_e = e_ref[...].reshape(rows, tokens)
+
+        def chip_rows(k, carry):
+            block = eall[r, pl.ds(k * 2 * group, 2 * group), lo:hi, :]
+            block = block.reshape(2 * group * size, tokens)
+            gram = token_product(block, own_e)
             cross = token_product(block, l_ref[...])
-            part[r, 0, q, 1] = cross[:sub]
-            part[r, 1, q, 1] = cross[sub:]
+            for g in range(group):
+                for core in range(2):
+                    at = (2 * g + core) * size
+                    part[r, core, k * group + g, 0, lo:hi] = gram[at : at + size]
+                    part[r, core, k * group + g, 1, lo:hi] = cross[at : at + size]
             return carry
 
-        lax.fori_loop(0, chips, chip_rows, 0)
-        sib_copy(r).start()
-
-    def finish(r):
-        sib_copy(r).wait_recv()
+        lax.fori_loop(0, chips // group, chip_rows, 0)
+        sib_copy(r, h).start()
+
+    def finish(r, h):
+        lo, hi = pieces[h]
+        sib_copy(r, h).wait_recv()
 
         def add(q, carry):
-            part[r, c, q] = part[r, c, q] + sib[r, q]
+            part[r, c, q, :, lo:hi] = part[r, c, q, :, lo:hi] + sib[r, q, :, lo:hi]
             return carry
 
         lax.fori_loop(0, chips, add, 0)
         for d in range(1, chips):
-            rs_copy(r, d).start()
+            rs_copy(r, h, d).start()
 
     def both(s, action):
         @pl.when(z - s >= 0)
@@ -164,28 +192,30 @@
             action(z + s)
 
     def level(s, carry):
-        both(s, lambda r: fetch(r, s == 0))
-        both(s, process)
+        both(s, lambda r: fetch(r, 0, s == 0))
+        both(s, lambda r: process(r, 0))
 
         @pl.when(s > 0)
         def _():
-            both(s - 1, finish)
-
+            both(s - 1, lambda r: finish(r, 1))
+
+        both(s, lambda r: fetch(r, 1, s == 0))
+        both(s, lambda r: process(r, 1))
+        both(s, lambda r: finish(r, 0))
         return carry
 
     lax.fori_loop(0, n_feat, level, 0)
-    both(n_feat - 1, finish)
-
-    col_abs = jnp.zeros((8, rows), f32)
-    diag = jnp.zeros((8, rows), f32)
+
+    stat[t] = jnp.zeros((8, rows), f32)
+
     row_id = lax.broadcasted_iota(jnp.int32, (sub, rows), 0)
     col_id = lax.broadcasted_iota(jnp.int32, (sub, rows), 1)
     on_diag = col_id == row_id + t * sub
 
-    def total(r, carry):
-        col_abs, diag = carry
-        for d in range(1, chips):
-            rs_copy(r, d).wait_recv()
+    def total(r):
+        for h in range(len(pieces)):
+            for d in range(1, chips):
+                rs_copy(r, h, d).wait_recv()
         both_sum = part[r, c, p]
         for d in range(1, chips):
             both_sum = both_sum + recv[d - 1, r]
@@ -193,19 +223,26 @@
         cbuf[r] = both_sum[1] / token_total
         high = gram.astype(bf16)
         gall[z, r] = high
+        for d in range(1, n_feat):
+            g_copy(r, d).start()
 
         @pl.when(r == z)
         def _():
             glow[z] = (gram - high.astype(f32)).astype(bf16)
-
-        col_abs = col_abs + jnp.sum(jnp.abs(gram).reshape(sub // 8, 8, rows), axis=0)
+            for d in range(1, n_feat):
+                gl_copy(d).start()
+
+        stat[t, 0:1] += jnp.sum(jnp.abs(gram), axis=0, keepdims=True)
         kept = jnp.where(on_diag, gram, 0.0) * jnp.where(r == z, 1.0, 0.0)
-        diag = diag + jnp.sum(kept.reshape(sub // 8, 8, rows), axis=0)
-        return col_abs, diag
-
-    col_abs, diag = lax.fori_loop(0, n_feat, total, (col_abs, diag))
-    stat[t, 0] = col_abs
-    stat[t, 1] = diag
+        stat[t, 1:2] += jnp.sum(kept, axis=0, keepdims=True)
+
+    def early(s, carry):
+        both(s, total)
+        return carry
+
+    lax.fori_loop(0, n_feat - 1, early, 0)
+    both(n_feat - 1, lambda r: finish(r, 1))
+    both(n_feat - 1, total)
 
     def st_copy(d):
         return remote(
@@ -213,18 +250,6 @@
             lax.rem(t + d, n_tok), z,
         )
 
-    def g_copy(d):
-        return remote(
-            gall.at[z], gall.at[z], g_ssem.at[d - 1], g_rsem.at[d - 1],
-            t, lax.rem(z + d, n_feat),
-        )
-
-    def gl_copy(d):
-        return remote(
-            glow.at[z], glow.at[z], gl_ssem.at[d - 1], gl_rsem.at[d - 1],
-            t, lax.rem(z + d, n_feat),
-        )
-
     def zs_copy(d):
         return remote(
             zstat.at[z], zstat.at[z], zs_ssem.at[d - 1], zs_rsem.at[d - 1],
@@ -236,16 +261,12 @@
     for d in range(1, n_tok):
         st_copy(d).wait_recv()
     tok_sum = jnp.sum(stat[...], axis=0)
-    sums = jnp.sum(tok_sum[0], axis=0, keepdims=True)
-    peak = jnp.max(sums, axis=1, keepdims=True)
-    trace = jnp.sum(jnp.sum(tok_sum[1], axis=0, keepdims=True), axis=1, keepdims=True)
+    peak = jnp.max(tok_sum[0:1], axis=1, keepdims=True)
+    trace = jnp.sum(tok_sum[1:2], axis=1, keepdims=True)
     zstat[z, 0] = jnp.broadcast_to(peak, (8, 128))
     zstat[z, 1] = jnp.broadcast_to(trace, (8, 128))
     for d in range(1, n_feat):
         zs_copy(d).start()
-    for d in range(1, n_feat):
-        g_copy(d).start()
-        gl_copy(d).start()
     for d in range(1, n_feat):
         zs_copy(d).wait_recv()
     seen = zstat[...]
@@ -289,7 +310,8 @@
             tf_copy(it, d).start()
         if it == 0:
             for d in range(1, n_feat):
-                g_copy(d).wait_recv()
+                for r in range(n_feat):
+                    g_copy(r, d).wait_recv()
                 gl_copy(d).wait_recv()
         for d in range(chips):
             tf_copy(it, d).wait_recv()
@@ -361,17 +383,20 @@
     out_ref[...] = outs[...]
 
     def drain(r, carry):
-        @pl.when(jnp.logical_and(r <= z, z < n_feat - 1))
-        def _():
-            up_copy(r).wait_send()
-
-        @pl.when(jnp.logical_and(r >= z, z > 0))
-        def _():
-            down_copy(r).wait_send()
-
-        sib_copy(r).wait_send()
-        for d in range(1, chips):
-            rs_copy(r, d).wait_send()
+        for h in range(len(pieces)):
+            @pl.when(jnp.logical_and(r <= z, z < n_feat - 1))
+            def _():
+                up_copy(r, h).wait_send()
+
+            @pl.when(jnp.logical_and(r >= z, z > 0))
+            def _():
+                down_copy(r, h).wait_send()
+
+            sib_copy(r, h).wait_send()
+            for d in range(1, chips):
+                rs_copy(r, h, d).wait_send()
+        for d in range(1, n_feat):
+            g_copy(r, d).wait_send()
         return carry
 
     lax.fori_loop(0, n_feat, drain, 0)
@@ -379,7 +404,6 @@
         st_copy(d).wait_send()
         fb_copy(d).wait_send()
     for d in range(1, n_feat):
-        g_copy(d).wait_send()
         gl_copy(d).wait_send()
         zs_copy(d).wait_send()
         fa_copy(d).wait_send()
@@ -403,7 +427,7 @@
         in_specs=[pl.BlockSpec(memory_space=pltpu.VMEM)] * 2,
         out_specs=pl.BlockSpec(memory_space=pltpu.VMEM),
         scratch_shapes=[
-            vmem((n_feat, rows, tokens), bf16),
+            vmem((n_feat, n_tok, sub, tokens), bf16),
             vmem((n_feat, 2, chips, 2, sub, rows), f32),
             vmem((n_feat, chips, 2, sub, rows), f32),
             vmem((chips - 1, n_feat, 2, sub, rows), f32),
@@ -413,16 +437,16 @@
             vmem(tile, f32),
             vmem(tile, f32),
             vmem((ITERS, n_feat, n_tok, sub, rows), bf16),
-            vmem((n_tok, 2, 8, rows), f32),
+            vmem((n_tok, 8, rows), f32),
             vmem((n_feat, 2, 8, 128), f32),
             vmem(tile, f32),
             vmem((n_tok, sub, width), f32),
             vmem((n_tok, sub, width), f32),
             dma,
-            dma((n_feat,)), dma((n_feat,)), dma((n_feat,)),
-            dma((n_feat,)), dma((n_feat,)),
-            dma((n_feat, chips - 1)), dma((n_feat, chips - 1)),
-            dma((n_feat - 1,)), dma((n_feat - 1,)),
+            dma((n_feat, 2)), dma((n_feat, 2)), dma((n_feat, 2)),
+            dma((n_feat, 2)), dma((n_feat, 2)),
+            dma((n_feat, 2, chips - 1)), dma((n_feat, 2, chips - 1)),
+            dma((n_feat, n_feat - 1)), dma((n_feat, n_feat - 1)),
             dma((n_feat - 1,)), dma((n_feat - 1,)),
             dma((n_tok - 1,)), dma((n_tok - 1,)),
             dma((n_feat - 1,)), dma((n_feat - 1,)),
@@ -434,7 +458,7 @@
         compiler_params=pltpu.CompilerParams(
             collective_id=0, has_side_effects=True, vmem_limit_bytes=VMEM_BYTES
         ),
-    )(entering, leaving)
+    )(entering.reshape(n_tok, sub, tokens), leaving)
     return out.reshape(rows, width)
 
 
@@ -445,7 +469,8 @@
         rows, tokens = entering.shape
         fits = (
             n_tok == 2 * n_feat
-            and rows % (16 * n_tok) == 0
+            and rows % (32 * n_tok) in (0, 16 * n_tok)
+            and rows // n_tok > 16
             and rows % 128 == 0
             and tokens % 128 == 0
         )

time: 237 us -> 225 us (0.949)
  Pallas kernels: 234 us -> 223 us
    pallas_call x1, Pallas kernels: 234 us -> 223 us  [kernel_body(): pl.pallas_call(functools.partial(kernel, n_tok, n_feat), out_shape=jax.Sh...]
where the time goes in v2:
time: 225 us
  Pallas kernels  223 us (99%)
  local copies, waits for them, and re-layouts  2.41 us (1%)
    pallas_call x1, Pallas kernels, kernel_body(): pl.pallas_call(functools.partial(kernel, n_tok, n_feat), out_shape=jax.Sh...  223 us

profile of v2, /device:TPU:9, one launch (start us, length us, event | category | flops | bytes accessed | tf_op | source)
XLA Modules:
  0.0 225.0 jit_solution(14357485754486549377)
XLA Ops:
  0.0 222.6 %shard_map.28 = f32[8,80,320]{2,1,0:T(8,128)} custom-call(bf16[8,80,1024]{2,1,0:T(8,128)(2,1)} %bitcast.3, bf16[640,1024]{1,0:T(8,128)(2,1)} %l_ref.1), custom_call_target="tpu_custom_call" | custom-call | tf_op jit(solution)/shard_map/pallas_call | solution.py:424
  222.6 2.4 %copy.3 = f32[640,320]{0,1:T(8,128)} copy(f32[640,320]{1,0:T(8,128)} %bitcast.2) | data formatting | bytes 1638400 | tf_op jit(solution)/shard_map/reshape | solution.py:462

commit v3 on v2

--- a/solution.py
+++ b/solution.py
@@ -212,6 +212,10 @@
     col_id = lax.broadcasted_iota(jnp.int32, (sub, rows), 1)
     on_diag = col_id == row_id + t * sub
 
+    def send_gram(r):
+        for d in range(1, n_feat):
+            g_copy(r, d).start()
+
     def total(r):
         for h in range(len(pieces)):
             for d in range(1, chips):
@@ -223,21 +227,21 @@
         cbuf[r] = both_sum[1] / token_total
         high = gram.astype(bf16)
         gall[z, r] = high
-        for d in range(1, n_feat):
-            g_copy(r, d).start()
 
         @pl.when(r == z)
         def _():
             glow[z] = (gram - high.astype(f32)).astype(bf16)
-            for d in range(1, n_feat):
-                gl_copy(d).start()
+
 
         stat[t, 0:1] += jnp.sum(jnp.abs(gram), axis=0, keepdims=True)
         kept = jnp.where(on_diag, gram, 0.0) * jnp.where(r == z, 1.0, 0.0)
         stat[t, 1:2] += jnp.sum(kept, axis=0, keepdims=True)
 
+    def total_send(r):
+        total(r)
+
     def early(s, carry):
-        both(s, total)
+        both(s, total_send)
         return carry
 
     lax.fori_loop(0, n_feat - 1, early, 0)
@@ -267,6 +271,10 @@
     zstat[z, 1] = jnp.broadcast_to(trace, (8, 128))
     for d in range(1, n_feat):
         zs_copy(d).start()
+    for r in range(n_feat):
+        send_gram(r)
+    for d in range(1, n_feat):
+        gl_copy(d).start()
     for d in range(1, n_feat):
         zs_copy(d).wait_recv()
     seen = zstat[...]
@@ -287,34 +295,50 @@
 
     lax.fori_loop(0, n_feat, start_iterate, 0)
 
-    def tg_copy(it, d):
-        dest = lax.rem(p + d, chips)
-        return remote(
-            tfull.at[it, :, t], tfull.at[it, :, t], tg_ssem.at[it, d - 1], tg_rsem.at[it, d - 1],
-            2 * dest + c, z,
-        )
-
-    def tf_copy(it, d):
-        tile = 2 * lax.rem(p + chips - d, chips) + c
-        return remote(
-            tfull.at[it, :, tile], tfull.at[it, :, tile], tf_ssem.at[it, d], tf_rsem.at[it, d],
-            mate, z,
-        )
+    beside = p + 1 - 2 * (p % 2)
+    across = p + 2 - 4 * (p // 2)
+    far = beside + 2 - 4 * (p // 2)
+    whole, low_half, high_half = slice(None), slice(0, n_feat // 2), slice(n_feat // 2, n_feat)
+    hops = (
+        (whole, t, beside), (whole, t, across),
+        (low_half, 2 * across + c, beside), (high_half, 2 * beside + c, across),
+    )
+    shares = (
+        (whole, t), (whole, 2 * beside + c), (whole, 2 * across + c),
+        (low_half, 2 * far + c), (high_half, 2 * far + c),
+    )
+
+    def tg_copy(it, k):
+        part_of, tile, dest = hops[k]
+        at = tfull.at[it, part_of, tile]
+        return remote(at, at, tg_ssem.at[it, k], tg_rsem.at[it, k], 2 * dest + c, z)
+
+    def tf_copy(it, k):
+        part_of, tile = shares[k]
+        at = tfull.at[it, part_of, tile]
+        return remote(at, at, tf_ssem.at[it, k], tf_rsem.at[it, k], mate, z)
 
     for it in range(ITERS):
-        for d in range(1, chips):
-            tg_copy(it, d).start()
+        tg_copy(it, 0).start()
+        tg_copy(it, 1).start()
         tf_copy(it, 0).start()
-        for d in range(1, chips):
-            tg_copy(it, d).wait_recv()
-            tf_copy(it, d).start()
+        tg_copy(it, 0).wait_recv()
+        tg_copy(it, 3).start()
+        tf_copy(it, 1).start()
+        tg_copy(it, 1).wait_recv()
+        tg_copy(it, 2).start()
+        tf_copy(it, 2).start()
+        tg_copy(it, 2).wait_recv()
+        tf_copy(it, 3).start()
+        tg_copy(it, 3).wait_recv()
+        tf_copy(it, 4).start()
         if it == 0:
             for d in range(1, n_feat):
                 for r in range(n_feat):
                     g_copy(r, d).wait_recv()
                 gl_copy(d).wait_recv()
-        for d in range(chips):
-            tf_copy(it, d).wait_recv()
+        for k in range(len(shares)):
+            tf_copy(it, k).wait_recv()
         ratio_next = 1.0 / (2.0 * center / half_span - ratio_now)
         keep = ratio_next * ratio_now
         gain = 2.0 * ratio_next / half_span
@@ -408,10 +432,10 @@
         zs_copy(d).wait_send()
         fa_copy(d).wait_send()
     for it in range(ITERS):
-        for d in range(1, chips):
-            tg_copy(it, d).wait_send()
-        for d in range(chips):
-            tf_copy(it, d).wait_send()
+        for k in range(len(hops)):
+            tg_copy(it, k).wait_send()
+        for k in range(len(shares)):
+            tf_copy(it, k).wait_send()
 
 
 def kernel_body(n_tok, n_feat, entering, leaving):
@@ -450,8 +474,8 @@
             dma((n_feat - 1,)), dma((n_feat - 1,)),
             dma((n_tok - 1,)), dma((n_tok - 1,)),
             dma((n_feat - 1,)), dma((n_feat - 1,)),
-            dma((ITERS, chips - 1)), dma((ITERS, chips - 1)),
-            dma((ITERS, chips)), dma((ITERS, chips)),
+            dma((ITERS, 4)), dma((ITERS, 4)),
+            dma((ITERS, 5)), dma((ITERS, 5)),
             dma((n_feat - 1,)), dma((n_feat - 1,)),
             dma((n_tok - 1,)), dma((n_tok - 1,)),
         ],
@@ -468,7 +492,8 @@
     def body(entering, leaving):
         rows, tokens = entering.shape
         fits = (
-            n_tok == 2 * n_feat
+            n_tok == 8
+            and n_feat == 4
             and rows % (32 * n_tok) in (0, 16 * n_tok)
             and rows // n_tok > 16
             and rows % 128 == 0

time: 225 us -> 213 us (0.947)
  Pallas kernels: 223 us -> 210 us
    pallas_call x1, Pallas kernels: 223 us -> 210 us  [kernel_body(): pl.pallas_call(functools.partial(kernel, n_tok, n_feat), out_shape=jax.Sh...]
where the time goes in v3:
time: 213 us; the launch traced here: 212 us
  Pallas kernels  210 us (99%)
  local copies, waits for them, and re-layouts  2.41 us (1%)
    pallas_call x1, Pallas kernels, kernel_body(): pl.pallas_call(functools.partial(kernel, n_tok, n_feat), out_shape=jax.Sh...  210 us

profile of v3, /device:TPU:9, one launch (start us, length us, event | category | flops | bytes accessed | tf_op | source)
XLA Modules:
  0.0 212.4 jit_solution(12525872851591872483)
XLA Ops:
  0.0 210.0 %shard_map.28 = f32[8,80,320]{2,1,0:T(8,128)} custom-call(bf16[8,80,1024]{2,1,0:T(8,128)(2,1)} %bitcast.3, bf16[640,1024]{1,0:T(8,128)(2,1)} %l_ref.1), custom_call_target="tpu_custom_call" | custom-call | tf_op jit(solution)/shard_map/pallas_call | solution.py:448
  210.0 2.4 %copy.3 = f32[640,320]{0,1:T(8,128)} copy(f32[640,320]{1,0:T(8,128)} %bitcast.2) | data formatting | bytes 1638400 | tf_op jit(solution)/shard_map/reshape | solution.py:486

commit v4 on v3

--- a/solution.py
+++ b/solution.py
@@ -239,12 +239,18 @@
 
     def total_send(r):
         total(r)
+        send_gram(r)
 
     def early(s, carry):
         both(s, total_send)
         return carry
 
-    lax.fori_loop(0, n_feat - 1, early, 0)
+    def later(s, carry):
+        both(s, total)
+        return carry
+
+    lax.fori_loop(0, 2, early, 0)
+    lax.fori_loop(2, n_feat - 1, later, 0)
     both(n_feat - 1, lambda r: finish(r, 1))
     both(n_feat - 1, total)
 
@@ -271,8 +277,12 @@
     zstat[z, 1] = jnp.broadcast_to(trace, (8, 128))
     for d in range(1, n_feat):
         zs_copy(d).start()
-    for r in range(n_feat):
-        send_gram(r)
+
+    def send_rest(s, carry):
+        both(s, send_gram)
+        return carry
+
+    lax.fori_loop(2, n_feat, send_rest, 0)
     for d in range(1, n_feat):
         gl_copy(d).start()
     for d in range(1, n_feat):
@@ -332,36 +342,28 @@
         tf_copy(it, 3).start()
         tg_copy(it, 3).wait_recv()
         tf_copy(it, 4).start()
-        if it == 0:
-            for d in range(1, n_feat):
-                for r in range(n_feat):
-                    g_copy(r, d).wait_recv()
-                gl_copy(d).wait_recv()
         for k in range(len(shares)):
             tf_copy(it, k).wait_recv()
         ratio_next = 1.0 / (2.0 * center / half_span - ratio_now)
         keep = ratio_next * ratio_now
         gain = 2.0 * ratio_next / half_span
 
-        def multiply(k, carry):
+        def multiply(d, k):
             weights = tfull[it, k].reshape(rows, rows)
             left = gall[k].reshape(n_feat * sub, rows)
             product = jnp.dot(left, weights, preferred_element_type=f32)
             low = jnp.dot(glow[k], weights, preferred_element_type=f32)
             product = product.reshape(n_feat, sub, rows)
 
-            @pl.when(k == 0)
-            def _():
-                fin[...] = product
-
-            @pl.when(k > 0)
-            def _():
-                fin[...] = fin[...] + product
-
+            fin[...] = product if d == 0 else fin[...] + product
             recv[0, k, 0] = low
-            return carry
-
-        lax.fori_loop(0, n_feat, multiply, 0)
+
+        for d in range(n_feat):
+            if it == 0 and d > 0:
+                for r in range(n_feat):
+                    g_copy(r, d).wait_recv()
+                gl_copy(d).wait_recv()
+            multiply(d, lax.rem(z + n_feat - d, n_feat))
 
         def advance(r, carry):
             applied = fin[r] + recv[0, r, 0]
@@ -384,24 +386,37 @@
             tbuf.at[dest], sib.at[0, z, 0], fa_ssem.at[d - 1], fa_rsem.at[d - 1], t, dest
         )
 
+    def fb_to(dest):
+        d = lax.rem(dest - t + n_tok, n_tok)
+        return remote(
+            halves.at[dest], outs.at[t], fb_ssem.at[d - 1], fb_rsem.at[d - 1], dest, z
+        )
+
     def fb_copy(d):
-        dest = lax.rem(t + d, n_tok)
-        return remote(
-            halves.at[dest], outs.at[t], fb_ssem.at[d - 1], fb_rsem.at[d - 1], dest, z
-        )
+        return fb_to(lax.rem(t + d, n_tok))
 
     for d in range(1, n_feat):
         fa_copy(d).start()
     sib[0, z, 0] = tbuf[z]
-    for d in range(1, n_feat):
-        fa_copy(d).wait_recv()
-    for k in range(n_feat):
+    def split(k):
         tile = sib[0, k, 0]
         halves[2 * k] = tile[:, :width]
         halves[2 * k + 1] = tile[:, width:]
-    for d in range(1, n_tok):
-        fb_copy(d).start()
-    outs[t] = halves[t]
+        for core in range(2):
+            dest = 2 * k + core
+
+            @pl.when(dest != t)
+            def _():
+                fb_to(dest).start()
+
+            @pl.when(dest == t)
+            def _():
+                outs[t] = halves[t]
+
+    split(z)
+    for d in range(1, n_feat):
+        fa_copy(d).wait_recv()
+        split(lax.rem(z + n_feat - d, n_feat))
     for d in range(1, n_tok):
         fb_copy(d).wait_recv()
     out_ref[...] = outs[...]

time: 213 us -> 203 us (0.953)
  Pallas kernels: 210 us -> 198 us
    pallas_call x1, Pallas kernels: 210 us -> 198 us  [kernel_body(): pl.pallas_call(functools.partial(kernel, n_tok, n_feat), out_shape=jax.Sh...]
where the time goes in v4:
time: 203 us; the launch traced here: 201 us
  Pallas kernels  198 us (98%)
  local copies, waits for them, and re-layouts  2.41 us (1%)
    pallas_call x1, Pallas kernels, kernel_body(): pl.pallas_call(functools.partial(kernel, n_tok, n_feat), out_shape=jax.Sh...  198 us

profile of v4, /device:TPU:9, one launch (start us, length us, event | category | flops | bytes accessed | tf_op | source)
XLA Modules:
  0.0 200.5 jit_solution(5757852813868151863)
XLA Ops:
  0.0 198.1 %shard_map.28 = f32[8,80,320]{2,1,0:T(8,128)} custom-call(bf16[8,80,1024]{2,1,0:T(8,128)(2,1)} %bitcast.3, bf16[640,1024]{1,0:T(8,128)(2,1)} %l_ref.1), custom_call_target="tpu_custom_call" | custom-call | tf_op jit(solution)/shard_map/pallas_call | solution.py:463
  198.1 2.4 %copy.3 = f32[640,320]{0,1:T(8,128)} copy(f32[640,320]{1,0:T(8,128)} %bitcast.2) | data formatting | bytes 1638400 | tf_op jit(solution)/shard_map/reshape | solution.py:501
